TPU v7x, 32 devices: a whole 2x2x4 slice. The times are simulated.
32 devices in a mesh: dom: 16 (over z, y, x), tgt: 2 (over core).
Axes of the slice: x: 2, y: 2, z: 4, core: 2. Of those that a mesh axis runs over, the one named last changes fastest.
Arguments:
- positions: float32 [3, 16384], P(None, ('dom', 'tgt')), may hold values from -3 to 3
- normals: float32 [3, 16384], P(None, ('dom', 'tgt')), may hold values from -6 to 6
- weights: float32 [16384], P(('dom', 'tgt')), may hold values from 0.001 to 0.01
- density: float32 [32, 16384], P(None, ('dom', 'tgt')), may hold values from -6 to 6
- partners: int32 [16, 8], P('dom'), may hold values from 0 to 15, as said below
- band_list: int32 [16, 8, 8], P('dom'), may hold values from 0 to 7
- near_list: int32 [128, 24], P(('dom', 'tgt')), may hold values from 0 to 71
- near_count: int32 [128], P(('dom', 'tgt')), may hold values from 1 to 24, as said below
- singular: int32 [128, 24], P(('dom', 'tgt')), may hold values 0 or 1
Outputs:
- near_field: float32 [32, 16384], P(None, ('dom', 'tgt'))
Inputs may be any that keep to these rules, and one draw needn't show every extreme that they name: In each matching the partners pair the partitions (the partner of a partner is the partition itself, never itself), and the 8 partners of a partition are distinct. `near_count`: 24 is reached by some target tile in every draw.
All inputs are finite; a program needn't handle non-finite values. No bound on the sum of `singular` on one device may be relied on, other than what follows from the above.
Results may differ from a plain program's by a relative error of at most 0.0041.
Values sent between devices are 32-bit elements; how exact they have to be, the bound alone decides.
A program may use at most 64 MiB of HBM per device.

v0:
```python
import math

import jax
import jax.numpy as jnp
from jax import lax
from jax.sharding import PartitionSpec as P

TILE = 128


wave_number = 6.0
coupling = 1.5
narrow_core = 0.1
wide_core = 0.4


def build_kernel(target_pos, source, valid_mask, flag_row):
    offset = source[:, 0:3, :, None] - target_pos[:, :, None, :]
    core_width = jnp.where(flag_row > 0, wide_core, narrow_core)[:, None, None]
    distance = jnp.sqrt(jnp.sum(offset * offset, axis=1) + core_width * core_width)
    inverse = 1.0 / distance
    normal_part = jnp.sum(offset * source[:, 3:6, :, None], axis=1) * inverse
    radial = inverse / (4.0 * math.pi)
    cos_part = jnp.cos(wave_number * distance) * radial
    sin_part = jnp.sin(wave_number * distance) * radial
    weight_mask = source[:, 6, :, None] * valid_mask[:, None, None]
    kernel_re = weight_mask * (
        normal_part * (-cos_part * inverse - wave_number * sin_part) - coupling * sin_part
    )
    kernel_im = weight_mask * (
        normal_part * (wave_number * cos_part - sin_part * inverse) + coupling * cos_part
    )
    return jnp.concatenate([kernel_re, kernel_im], axis=1).astype(jnp.bfloat16)


def density_side(source):
    density_bf = source[:, 7:, :].astype(jnp.bfloat16)
    half_rows = density_bf.shape[1] // 2
    real_part = density_bf[:, :half_rows]
    imag_part = density_bf[:, half_rows:]
    upper = jnp.concatenate([real_part, -imag_part], axis=2)
    lower = jnp.concatenate([imag_part, real_part], axis=2)
    return jnp.concatenate([upper, lower], axis=1)


def shards(
    positions, normals, weights, density, partners, band_list, near_list, near_count, singular
):
    payload = jnp.concatenate([positions, normals, weights[None, :], density], axis=0)
    channels = payload.shape[0]
    local_tiles = payload.shape[1] // TILE
    whole_part = lax.all_gather(payload, "tgt", axis=1, tiled=True)
    part_tiles = whole_part.reshape(channels, -1, TILE).transpose(1, 0, 2)
    n_dom = lax.axis_size("dom")
    band_size = band_list.shape[2]
    my_partners = partners[0]
    send_slots = jnp.zeros((n_dom, band_size, channels, TILE), jnp.float32)
    send_slots = send_slots.at[my_partners].set(part_tiles[band_list[0]])
    arrived = lax.all_to_all(send_slots, "dom", split_axis=0, concat_axis=0, tiled=True)
    band_tiles = arrived[my_partners]
    source_pool = jnp.concatenate([part_tiles, band_tiles.reshape(-1, channels, TILE)], axis=0)
    target_pos = positions.reshape(3, local_tiles, TILE).transpose(1, 0, 2)
    pair_targets = jnp.concatenate([target_pos, target_pos], axis=0)

    def add_pair(pair_idx, totals):
        columns = lax.dynamic_slice_in_dim(near_list, 2 * pair_idx, 2, 1)
        flag_pair = lax.dynamic_slice_in_dim(singular, 2 * pair_idx, 2, 1)
        pick_idx = columns.T.reshape(-1)
        source = source_pool[pick_idx]
        entry_ids = 2 * pair_idx + jnp.arange(2, dtype=jnp.int32)
        valid_mask = (entry_ids[:, None] < near_count[None, :]).reshape(-1).astype(jnp.float32)
        kernel = build_kernel(pair_targets, source, valid_mask, flag_pair.T.reshape(-1))
        left_side = density_side(source)
        term_pairs = jnp.einsum(
            "brs,bst->brt", left_side, kernel, preferred_element_type=jnp.float32
        )
        return totals + term_pairs[:local_tiles] + term_pairs[local_tiles:]

    trip_count = (jnp.max(near_count) + 1) // 2
    start_sum = jnp.zeros((local_tiles, channels - 7, TILE), jnp.float32)
    totals = lax.fori_loop(0, trip_count, add_pair, start_sum)
    return totals.transpose(1, 0, 2).reshape(channels - 7, local_tiles * TILE)


def solution(mesh):
    in_specs = (
        P(None, ("dom", "tgt")),
        P(None, ("dom", "tgt")),
        P(("dom", "tgt")),
        P(None, ("dom", "tgt")),
        P("dom", None),
        P("dom", None, None),
        P(("dom", "tgt"), None),
        P(("dom", "tgt")),
        P(("dom", "tgt"), None),
    )
    out_specs = P(None, ("dom", "tgt"))
    return jax.shard_map(shards, mesh=mesh, in_specs=in_specs, out_specs=out_specs, check_vma=False)
```

profile of v0, /device:TPU:21, one launch (start us, length us, event | category | flops | bytes accessed | tf_op | source)
XLA Modules:
  0.0 138.0 jit_solution(14776132372673987182)
XLA Ops:
  0.9 2.2 %all_gather.3 = f32[39,1024]{1,0:T(8,128)S(1)} all-gather(f32[39,512]{1,0:T(8,128)S(1)} %pad_maximum_fusion.1), channel_id=1, replica_groups=mesh['dom'=16,'tgt'=2] {'tgt'}, dimensions={1}, use_global_device_ids=true | all-gather | bytes 239616 | tf_op jit(solution)/shard_map/all_gather | solution.py:52
  4.7 1.6 %broadcast_in_dim.16 = f32[16,8,39,128]{3,1,2,0:T(8,128)} broadcast(f32[]{:T(128)} %constant.16.clone.1), dimensions={} | broadcast | bytes 2555908 | tf_op jit(solution)/shard_map/broadcast_in_dim | solution.py:57
  6.3 3.1 %scatter_fusion = f32[16,8,39,128]{3,1,2,0:T(8,128)} fusion(f32[16,8,39,128]{3,1,2,0:T(8,128)} %broadcast_in_dim.16, s32[8]{0:T(128)S(1)} %fusion.19, f32[8,8,39,128]{3,1,2,0:T(8,128)S(1)} %copy.29), kind=kCustom, calls=%fused_computation.3 | custom fusion | bytes 3833888 | tf_op jit(solution)/shard_map/scatter | solution.py:58
  9.4 6.7 %all-to-all-start = ((f32[16,8,39,128]{3,1,2,0:T(8,128)}), f32[16,8,39,128]{3,1,2,0:T(8,128)S(1)}, u32[]{:S(2)}, u32[]{:S(2)}) async-start(f32[16,8,39,128]{3,1,2,0:T(8,128)} %scatter_fusion), calls=%async_computation | async-start | bytes 5111808 | tf_op jit(solution)/shard_map/all_to_all | solution.py:59
  17.6 54.6 %all-to-all-done = f32[16,8,39,128]{3,1,2,0:T(8,128)S(1)} async-done(((f32[16,8,39,128]{3,1,2,0:T(8,128)}), f32[16,8,39,128]{3,1,2,0:T(8,128)S(1)}, u32[]{:S(2)}, u32[]{:S(2)}) %all-to-all-start) | async-done | bytes 2555936 | tf_op jit(solution)/shard_map/all_to_all | solution.py:59
  72.2 1.7 %gather_fusion.2 = f32[8,8,39,128]{3,1,2,0:T(8,128)} fusion(f32[16,8,39,128]{3,1,2,0:T(8,128)S(1)} %all-to-all-done, s32[1024]{0:T(1024)S(1)} %pad_clamp_fusion.1), kind=kCustom, calls=%fused_computation.2 | custom fusion | bytes 2555936 | tf_op jit(solution)/shard_map/gather | solution.py:60
  73.9 1.5 %copy.42 = f32[8,8,39,128]{3,1,0,2:T(8,128)S(1)} copy(f32[8,8,39,128]{3,1,2,0:T(8,128)} %gather_fusion.2) | data formatting | bytes 2555904 | tf_op jit(solution)/shard_map/gather | solution.py:60
  75.7 61.6 %while.10 = (s32[]{:T(128)}, f32[4,32,128]{2,1,0:T(8,128)S(1)}, s32[]{:T(128)}, s32[4,24]{0,1:T(8,128)S(1)}, f32[72,39,128]{2,1,0:T(8,128)S(1)}, /*index=5*/s32[...) while((s32[]{:T(128)}, f32[4,32,128]{2,1,0:T(8,128)S(1)}, ...), condition=%wide.region_5.6_spmd, body=%wide.region_2.5_spmd.sunk | while | flops 23290952 | bytes 4471535 | solution.py:81
  77.9 2.7 %multiply_convert_fusion.3 = (bf16[8,128,128]{2,1,0:T(8,128)(2,1)S(1)}, bf16[8,128,128]{2,1,0:T(8,128)(2,1)S(1)}) fusion(f32[8,128,128]{2,1,0:T(8,128)S(1)} %get-tuple-element.169, f32[8,128,128]{2,1,0:T(8,128)S(1)} %get-tuple-element.170, f32[8]{0:T(128)S(1)} %mul.168, f32[8,128]{1,0:T(8,128)S(1)} %broadcast_multiply_fusion.2), kind=kLoop, calls=%fused_computation.13.clone.1 | loop fusion | flops 3145728 | bytes 1576992 | tf_op jit(solution)/shard_map/convert.1
  83.0 2.7 %multiply_convert_fusion.3 = (bf16[8,128,128]{2,1,0:T(8,128)(2,1)S(1)}, bf16[8,128,128]{2,1,0:T(8,128)(2,1)S(1)}) fusion(f32[8,128,128]{2,1,0:T(8,128)S(1)} %get-tuple-element.169, f32[8,128,128]{2,1,0:T(8,128)S(1)} %get-tuple-element.170, f32[8]{0:T(128)S(1)} %mul.168, f32[8,128]{1,0:T(8,128)S(1)} %broadcast_multiply_fusion.2), kind=kLoop, calls=%fused_computation.13.clone.1 | loop fusion | flops 3145728 | bytes 1576992 | tf_op jit(solution)/shard_map/convert.1
  86.7 1.0 fusion.33
  88.1 2.7 %multiply_convert_fusion.3 = (bf16[8,128,128]{2,1,0:T(8,128)(2,1)S(1)}, bf16[8,128,128]{2,1,0:T(8,128)(2,1)S(1)}) fusion(f32[8,128,128]{2,1,0:T(8,128)S(1)} %get-tuple-element.169, f32[8,128,128]{2,1,0:T(8,128)S(1)} %get-tuple-element.170, f32[8]{0:T(128)S(1)} %mul.168, f32[8,128]{1,0:T(8,128)S(1)} %broadcast_multiply_fusion.2), kind=kLoop, calls=%fused_computation.13.clone.1 | loop fusion | flops 3145728 | bytes 1576992 | tf_op jit(solution)/shard_map/convert.1
  93.3 2.7 %multiply_convert_fusion.3 = (bf16[8,128,128]{2,1,0:T(8,128)(2,1)S(1)}, bf16[8,128,128]{2,1,0:T(8,128)(2,1)S(1)}) fusion(f32[8,128,128]{2,1,0:T(8,128)S(1)} %get-tuple-element.169, f32[8,128,128]{2,1,0:T(8,128)S(1)} %get-tuple-element.170, f32[8]{0:T(128)S(1)} %mul.168, f32[8,128]{1,0:T(8,128)S(1)} %broadcast_multiply_fusion.2), kind=kLoop, calls=%fused_computation.13.clone.1 | loop fusion | flops 3145728 | bytes 1576992 | tf_op jit(solution)/shard_map/convert.1
  98.4 2.7 %multiply_convert_fusion.3 = (bf16[8,128,128]{2,1,0:T(8,128)(2,1)S(1)}, bf16[8,128,128]{2,1,0:T(8,128)(2,1)S(1)}) fusion(f32[8,128,128]{2,1,0:T(8,128)S(1)} %get-tuple-element.169, f32[8,128,128]{2,1,0:T(8,128)S(1)} %get-tuple-element.170, f32[8]{0:T(128)S(1)} %mul.168, f32[8,128]{1,0:T(8,128)S(1)} %broadcast_multiply_fusion.2), kind=kLoop, calls=%fused_computation.13.clone.1 | loop fusion | flops 3145728 | bytes 1576992 | tf_op jit(solution)/shard_map/convert.1
  103.5 2.7 %multiply_convert_fusion.3 = (bf16[8,128,128]{2,1,0:T(8,128)(2,1)S(1)}, bf16[8,128,128]{2,1,0:T(8,128)(2,1)S(1)}) fusion(f32[8,128,128]{2,1,0:T(8,128)S(1)} %get-tuple-element.169, f32[8,128,128]{2,1,0:T(8,128)S(1)} %get-tuple-element.170, f32[8]{0:T(128)S(1)} %mul.168, f32[8,128]{1,0:T(8,128)S(1)} %broadcast_multiply_fusion.2), kind=kLoop, calls=%fused_computation.13.clone.1 | loop fusion | flops 3145728 | bytes 1576992 | tf_op jit(solution)/shard_map/convert.1
  107.3 1.0 fusion.33
  108.7 2.7 %multiply_convert_fusion.3 = (bf16[8,128,128]{2,1,0:T(8,128)(2,1)S(1)}, bf16[8,128,128]{2,1,0:T(8,128)(2,1)S(1)}) fusion(f32[8,128,128]{2,1,0:T(8,128)S(1)} %get-tuple-element.169, f32[8,128,128]{2,1,0:T(8,128)S(1)} %get-tuple-element.170, f32[8]{0:T(128)S(1)} %mul.168, f32[8,128]{1,0:T(8,128)S(1)} %broadcast_multiply_fusion.2), kind=kLoop, calls=%fused_computation.13.clone.1 | loop fusion | flops 3145728 | bytes 1576992 | tf_op jit(solution)/shard_map/convert.1
  112.4 1.0 fusion.33
  113.8 2.7 %multiply_convert_fusion.3 = (bf16[8,128,128]{2,1,0:T(8,128)(2,1)S(1)}, bf16[8,128,128]{2,1,0:T(8,128)(2,1)S(1)}) fusion(f32[8,128,128]{2,1,0:T(8,128)S(1)} %get-tuple-element.169, f32[8,128,128]{2,1,0:T(8,128)S(1)} %get-tuple-element.170, f32[8]{0:T(128)S(1)} %mul.168, f32[8,128]{1,0:T(8,128)S(1)} %broadcast_multiply_fusion.2), kind=kLoop, calls=%fused_computation.13.clone.1 | loop fusion | flops 3145728 | bytes 1576992 | tf_op jit(solution)/shard_map/convert.1
  118.9 2.7 %multiply_convert_fusion.3 = (bf16[8,128,128]{2,1,0:T(8,128)(2,1)S(1)}, bf16[8,128,128]{2,1,0:T(8,128)(2,1)S(1)}) fusion(f32[8,128,128]{2,1,0:T(8,128)S(1)} %get-tuple-element.169, f32[8,128,128]{2,1,0:T(8,128)S(1)} %get-tuple-element.170, f32[8]{0:T(128)S(1)} %mul.168, f32[8,128]{1,0:T(8,128)S(1)} %broadcast_multiply_fusion.2), kind=kLoop, calls=%fused_computation.13.clone.1 | loop fusion | flops 3145728 | bytes 1576992 | tf_op jit(solution)/shard_map/convert.1
  124.1 2.7 %multiply_convert_fusion.3 = (bf16[8,128,128]{2,1,0:T(8,128)(2,1)S(1)}, bf16[8,128,128]{2,1,0:T(8,128)(2,1)S(1)}) fusion(f32[8,128,128]{2,1,0:T(8,128)S(1)} %get-tuple-element.169, f32[8,128,128]{2,1,0:T(8,128)S(1)} %get-tuple-element.170, f32[8]{0:T(128)S(1)} %mul.168, f32[8,128]{1,0:T(8,128)S(1)} %broadcast_multiply_fusion.2), kind=kLoop, calls=%fused_computation.13.clone.1 | loop fusion | flops 3145728 | bytes 1576992 | tf_op jit(solution)/shard_map/convert.1
  129.2 2.7 %multiply_convert_fusion.3 = (bf16[8,128,128]{2,1,0:T(8,128)(2,1)S(1)}, bf16[8,128,128]{2,1,0:T(8,128)(2,1)S(1)}) fusion(f32[8,128,128]{2,1,0:T(8,128)S(1)} %get-tuple-element.169, f32[8,128,128]{2,1,0:T(8,128)S(1)} %get-tuple-element.170, f32[8]{0:T(128)S(1)} %mul.168, f32[8,128]{1,0:T(8,128)S(1)} %broadcast_multiply_fusion.2), kind=kLoop, calls=%fused_computation.13.clone.1 | loop fusion | flops 3145728 | bytes 1576992 | tf_op jit(solution)/shard_map/convert.1
  133.0 1.0 fusion.33
  134.4 2.7 %multiply_convert_fusion.3 = (bf16[8,128,128]{2,1,0:T(8,128)(2,1)S(1)}, bf16[8,128,128]{2,1,0:T(8,128)(2,1)S(1)}) fusion(f32[8,128,128]{2,1,0:T(8,128)S(1)} %get-tuple-element.169, f32[8,128,128]{2,1,0:T(8,128)S(1)} %get-tuple-element.170, f32[8]{0:T(128)S(1)} %mul.168, f32[8,128]{1,0:T(8,128)S(1)} %broadcast_multiply_fusion.2), kind=kLoop, calls=%fused_computation.13.clone.1 | loop fusion | flops 3145728 | bytes 1576992 | tf_op jit(solution)/shard_map/convert.1
  (243 shorter events, 27.9 us)
Async XLA Ops:
  0.0 3.2 %copy-start.2 = (s32[1,8,8]{2,1,0:T(8,128)S(1)}, s32[1,8,8]{2,1,0:T(8,128)}, u32[]{:S(2)}) copy-start(s32[1,8,8]{2,1,0:T(8,128)} %param.16) | copy-start | bytes 772
  4.0 0.7 copy-start.5
  9.4 6.7 %copy-start.1 = (s32[4]{0:T(128)S(1)}, s32[4]{0:T(128)}, u32[]{:S(2)}) copy-start(s32[4]{0:T(128)} %param.18) | copy-start | bytes 52
  9.4 8.0 %copy-start.3 = (s32[4,24]{1,0:T(4,128)S(1)}, s32[4,24]{1,0:T(4,128)}, u32[]{:S(2)}) copy-start(s32[4,24]{1,0:T(4,128)} %param.17) | copy-start | bytes 1156
  9.4 8.1 %copy-start.4 = (s32[4,24]{1,0:T(4,128)S(1)}, s32[4,24]{1,0:T(4,128)}, u32[]{:S(2)}) copy-start(s32[4,24]{1,0:T(4,128)} %param.19) | copy-start | bytes 1156
  9.4 8.2 %copy-start = (f32[3,512]{1,0:T(4,128)S(1)}, f32[3,512]{1,0:T(4,128)}, u32[]{:S(2)}) copy-start(f32[3,512]{1,0:T(4,128)} %param.11) | copy-start | bytes 18436
  9.4 62.8 %all-to-all-start = ((f32[16,8,39,128]{3,1,2,0:T(8,128)}), f32[16,8,39,128]{3,1,2,0:T(8,128)S(1)}, u32[]{:S(2)}, u32[]{:S(2)}) async-start(f32[16,8,39,128]{3,1,2,0:T(8,128)} %scatter_fusion), calls=%async_computation | async-start | bytes 5111808 | tf_op jit(solution)/shard_map/all_to_all | solution.py:59
where the time goes:
time: 139 us; the launch traced here: 138 us
  waiting for transfers between devices  54.6 us (39%)
  other arithmetic  49.6 us (36%)
  local copies, waits for them, and re-layouts  20.4 us (15%)
  starting transfers between devices  6.65 us (5%)
  matrix products  2.39 us (2%)
  blocking collectives  2.24 us (2%)
    all_to_all x1, waiting for transfers between devices, shards(): lax.all_to_all(send_slots, 'dom', split_axis=0, concat_axis=0, tiled=True)  54.6 us
    another operation x24, other arithmetic  32.7 us
    reduce_sum x12, other arithmetic, build_kernel(): normal_part = jnp.sum(offset * source[:, 3:6, :, None], axis=1) * inverse  12.4 us
    gather x12, local copies, waits for them, and re-layouts, add_pair(): source = source_pool[pick_idx]  6.7 us
    all_to_all x1, starting transfers between devices, shards(): lax.all_to_all(send_slots, 'dom', split_axis=0, concat_axis=0, tiled=True)  6.65 us
    gather x2, local copies, waits for them, and re-layouts, shards(): band_tiles = arrived[my_partners]  3.14 us
    scatter x1, local copies, waits for them, and re-layouts, shards(): send_slots = send_slots.at[my_partners].set(part_tiles[band_list[0]])  3.05 us
  transfers between devices with their start and end apart: 1, of which 1 were waited for; matrix products, arithmetic and copies ran while one was open for 1% of the time, Pallas kernels for 0%

commit v1 on v0

v1 whole, which is shorter than its diff:
```python
import functools
import math

import jax
import jax.numpy as jnp
from jax import lax
from jax.experimental import pallas as pl
from jax.experimental.pallas import tpu as pltpu
from jax.sharding import PartitionSpec as P

TILE = 128
CHUNK = 32

wave_number = 6.0
coupling = 1.5
narrow_core = 0.1
wide_core = 0.4

SIN_POLY = (4.442882919124345, -7.308245686509064, 3.606354218433074, -0.8461116503755194, 0.10982451642926026)
COS_POLY = (1.4142134962552286, -6.978850948563789, 5.73946037690675, -1.8835579059841712, 0.3106880275217573)


def poly(coefs, z):
    total = coefs[-1]
    for c in coefs[-2::-1]:
        total = total * z + c
    return total


def gather_kernel(
    columns, depth, own_ref, all_ref, z_recv, a_recv, b_recv, s_recv, up_send, down_send, a_send, b_send, s_send, own_sem
):
    mesh_id = pl.DeviceIdType.MESH
    dom, core = lax.axis_index("dom"), lax.axis_index("tgt")
    x, y, z = dom % 2, (dom // 2) % 2, dom // 4
    half = own_ref.shape[-1] // 2
    flip = ((2 * y + 1 - x), (2 * (1 - y) + x))
    place = (2 * y + x, flip[0], flip[1], 2 * (1 - y) + 1 - x)

    def part(ref, block, h):
        return ref.at[block, :, pl.ds(h * half, half)]

    def block_of(c, zz):
        return (4 * zz + place[c]) * 2 + core

    barrier = pltpu.get_barrier_semaphore()
    peers = (((4 * z + flip[0]), core), ((4 * z + flip[1]), core), (dom, 1 - core))
    for peer in peers:
        pl.semaphore_signal(barrier, inc=1, device_id=peer, device_id_type=mesh_id)

    @pl.when(z > 0)
    def _():
        pl.semaphore_signal(barrier, inc=1, device_id=(dom - 4, core), device_id_type=mesh_id)

    @pl.when(z < depth - 1)
    def _():
        pl.semaphore_signal(barrier, inc=1, device_id=(dom + 4, core), device_id_type=mesh_id)

    own_copy = pltpu.make_async_copy(own_ref.at[0], all_ref.at[dom * 2 + core], own_sem)
    own_copy.start()
    inner = jnp.logical_and(z > 0, z < depth - 1)

    @pl.when(inner)
    def _():
        pl.semaphore_wait(barrier, 5)

    @pl.when(jnp.logical_not(inner))
    def _():
        pl.semaphore_wait(barrier, 4)

    def remote(src, dst, send, recv, device):
        return pltpu.make_async_remote_copy(
            src_ref=src, dst_ref=dst, send_sem=send, recv_sem=recv, device_id=device, device_id_type=mesh_id
        )

    def source(c, zz, h, own):
        return part(own_ref, 0, h) if own else part(all_ref, block_of(c, zz), h)

    def z_copy(zz, h, step, own):
        send = (up_send if step > 0 else down_send).at[h, zz]
        return remote(
            source(0, zz, h, own), part(all_ref, block_of(0, zz), h), send, z_recv.at[h, zz], (dom + 4 * step, core)
        )

    def a_copy(zz, h, own):
        peer = peers[0] if h == 0 else peers[1]
        return remote(
            source(0, zz, h, own), part(all_ref, block_of(0, zz), h), a_send.at[h, zz], a_recv.at[h, zz], peer
        )

    def b_copy(c, zz, h, own):
        peer = peers[1] if h == 0 else peers[0]
        col = 0 if c == 0 else (1 if h == 0 else 2)
        return remote(
            source(col, zz, h, own),
            part(all_ref, block_of(col, zz), h),
            b_send.at[h, c, zz],
            b_recv.at[h, c, zz],
            peer,
        )

    def s_copy(c, zz, h, own):
        return remote(
            source(c, zz, h, own),
            part(all_ref, block_of(c, zz), h),
            s_send.at[h, c, zz],
            s_recv.at[h, c, zz],
            peers[2],
        )

    levels = [[0]] + [[-k, k] for k in range(1, depth)]

    def each(level, body):
        for step in levels[level]:
            zz = z + step
            if step == 0:
                body(zz, 0)
            elif step < 0:
                pl.when(zz >= 0)(functools.partial(body, zz, step))
            else:
                pl.when(zz < depth)(functools.partial(body, zz, step))

    def along_z(zz, step):
        own = step == 0
        for h in range(2):
            if not own:
                z_copy(zz, h, 1, False).wait_recv()
            if step <= 0:

                @pl.when(z < depth - 1)
                def _(h=h):
                    z_copy(zz, h, 1, own).start()

            if step >= 0:

                @pl.when(z > 0)
                def _(h=h):
                    z_copy(zz, h, -1, own).start()

            a_copy(zz, h, own).start()
            b_copy(0, zz, h, own).start()
            s_copy(0, zz, h, own).start()

    def from_a(zz, step):
        for h in range(2):
            a_copy(zz, h, False).wait_recv()
            b_copy(1, zz, h, False).start()
            s_copy(1 if h == 0 else 2, zz, h, False).start()

    def from_b(zz, step):
        for h in range(2):
            b_copy(0, zz, h, False).wait_recv()
            s_copy(2 if h == 0 else 1, zz, h, False).start()

    def from_ab(zz, step):
        for h in range(2):
            b_copy(1, zz, h, False).wait_recv()
            s_copy(3, zz, h, False).start()

    for turn in range(depth + 2):
        if turn < depth:
            each(turn, along_z)
        if 1 <= turn <= depth:
            each(turn - 1, from_a)
            each(turn - 1, from_b)
        if turn >= 2:
            each(turn - 2, from_ab)

    own_copy.wait()

    def finish(zz, step):
        for h in range(2):
            if step <= 0:

                @pl.when(z < depth - 1)
                def _(h=h):
                    z_copy(zz, h, 1, False).wait_send()

            if step >= 0:

                @pl.when(z > 0)
                def _(h=h):
                    z_copy(zz, h, -1, False).wait_send()

            a_copy(zz, h, False).wait_send()
            for c in range(2):
                b_copy(c, zz, h, False).wait_send()
            for c in range(4):
                s_copy(c, zz, h, False).wait()

    for level in range(depth):
        each(level, finish)


def gather_blocks(payload, n_dom, n_tgt):
    channels, points = payload.shape
    if n_tgt != 2 or n_dom % 4 or n_dom > 16 or points % (2 * TILE):
        return lax.all_gather(payload, ("dom", "tgt"), axis=0, tiled=False)
    depth = n_dom // 4
    dma = pltpu.SemaphoreType.DMA
    return pl.pallas_call(
        functools.partial(gather_kernel, n_dom, depth),
        out_shape=jax.ShapeDtypeStruct((n_dom * n_tgt, channels, points), jnp.float32),
        in_specs=[pl.BlockSpec(memory_space=pltpu.VMEM)],
        out_specs=pl.BlockSpec(memory_space=pltpu.VMEM),
        scratch_shapes=[
            dma((2, depth)),
            dma((2, depth)),
            dma((2, 2, depth)),
            dma((2, 4, depth)),
            dma((2, depth)),
            dma((2, depth)),
            dma((2, depth)),
            dma((2, 2, depth)),
            dma((2, 4, depth)),
            dma,
        ],
        compiler_params=pltpu.CompilerParams(collective_id=0, has_side_effects=True),
    )(payload[None])


def entry_kernel(
    n_tgt, rhs2, near_ref, count_ref, flag_ref, partner_ref, band_ref, own_ref, all_ref, out_ref, xb, kbuf, left
):
    local_tiles, max_near = near_ref.shape
    band_size = band_ref.shape[1] // partner_ref.shape[1]
    part_tiles = local_tiles * n_tgt
    me = lax.axis_index("dom")
    half_rows = rhs2 // 2
    kbuf[...] = jnp.zeros_like(kbuf)

    def one_tile(t, _):
        lanes = pl.ds(pl.multiple_of(t * TILE, TILE), TILE)
        for c in range(3):
            row = own_ref[pl.ds(rhs2 + c, 1), lanes]
            xb[c] = jnp.broadcast_to(row, (TILE, TILE)).T
        used = count_ref[t]
        left[...] = jnp.zeros_like(left)

        def locate(j):
            pick = near_ref[t, j]
            beyond = jnp.maximum(pick - part_tiles, 0)
            other = partner_ref[0, beyond // band_size]
            far_tile = band_ref[other, beyond]
            is_own = pick < part_tiles
            tile = jnp.where(is_own, pick, far_tile)
            dom = jnp.where(is_own, me, other)
            return dom * n_tgt + tile // local_tiles, tile % local_tiles

        def add_pair(i, total):
            total = total + lax.dot_general(
                left[...], kbuf[...], (((1,), (1,)), ((), ())), preferred_element_type=jnp.float32
            )
            for e in range(2):
                j = 2 * i + e
                jj = jnp.minimum(j, max_near - 1)
                block, tile = locate(jj)
                core = jnp.where(flag_ref[t, jj] > 0, wide_core, narrow_core) * wave_number
                core_sq = core * core
                valid = jnp.where(j < used, 1.0, 0.0)
                cols = pl.ds(pl.multiple_of(tile * TILE, TILE), TILE)
                real = all_ref[block, pl.ds(0, half_rows), cols]
                imag = all_ref[block, pl.ds(half_rows, half_rows), cols]
                base = 2 * TILE * e
                left[:half_rows, base : base + TILE] = (-real).astype(jnp.bfloat16)
                left[:half_rows, base + TILE : base + 2 * TILE] = (-imag).astype(jnp.bfloat16)
                left[half_rows:, base : base + TILE] = (-imag).astype(jnp.bfloat16)
                left[half_rows:, base + TILE : base + 2 * TILE] = real.astype(jnp.bfloat16)
                rows = [
                    jnp.broadcast_to(all_ref[block, pl.ds(rhs2 + c, 1), cols], (CHUNK, TILE)) for c in range(7)
                ]
                weight = rows[6] * valid
                for k in range(TILE // CHUNK):
                    part = pl.ds(k * CHUNK, CHUNK)
                    dx = rows[0] - xb[0, part]
                    dy = rows[1] - xb[1, part]
                    dz = rows[2] - xb[2, part]
                    d_sq = (dx * dx + core_sq) + (dy * dy + dz * dz)
                    along = dx * rows[3] + dy * rows[4] + dz * rows[5]
                    inverse = lax.rsqrt(d_sq)
                    turns = d_sq * (inverse * (0.5 / math.pi))
                    frac = turns - jnp.round(turns)
                    z = frac * frac
                    s = frac * poly(SIN_POLY, z)
                    sin = s * poly(COS_POLY, z)
                    cos = 1.0 - s * s
                    slope = along * inverse
                    radial = inverse * weight
                    a = slope * inverse * radial
                    b = (slope + coupling) * radial
                    kbuf[part, base : base + TILE] = (cos * a + sin * b).astype(jnp.bfloat16)
                    kbuf[part, base + TILE : base + 2 * TILE] = (cos * b - sin * a).astype(jnp.bfloat16)
            return total

        total = lax.fori_loop(0, (used + 1) // 2, add_pair, jnp.zeros((rhs2, TILE), jnp.float32))
        total = total + lax.dot_general(
            left[...], kbuf[...], (((1,), (1,)), ((), ())), preferred_element_type=jnp.float32
        )
        out_ref[:, lanes] = total
        return 0

    lax.fori_loop(0, local_tiles, one_tile, 0)


def shards(
    positions, normals, weights, density, partners, band_list, near_list, near_count, singular
):
    n_dom, n_tgt = lax.axis_size("dom"), lax.axis_size("tgt")
    points = positions.shape[1]
    rhs2 = density.shape[0]
    rounds, band_size = band_list.shape[1:]
    bands = rounds * band_size
    band_row = jnp.pad(band_list.reshape(1, bands).astype(jnp.float32), ((0, 0), (0, points - bands)))
    payload = jnp.concatenate(
        [
            density,
            positions * wave_number,
            normals * wave_number,
            weights[None, :] * (wave_number / (4.0 * math.pi)),
            band_row,
        ],
        axis=0,
    )
    blocks = gather_blocks(payload, n_dom, n_tgt)
    bands_all = blocks[::n_tgt, rhs2 + 7, :bands].astype(jnp.int32)
    smem = pl.BlockSpec(memory_space=pltpu.SMEM)
    vmem = pl.BlockSpec(memory_space=pltpu.VMEM)
    return pl.pallas_call(
        functools.partial(entry_kernel, n_tgt, rhs2),
        out_shape=jax.ShapeDtypeStruct((rhs2, points), jnp.float32),
        in_specs=[smem] * 5 + [vmem] * 2,
        out_specs=vmem,
        scratch_shapes=[
            pltpu.VMEM((3, TILE, TILE), jnp.float32),
            pltpu.VMEM((TILE, 4 * TILE), jnp.bfloat16),
            pltpu.VMEM((rhs2, 4 * TILE), jnp.bfloat16),
        ],
    )(near_list, near_count, singular, partners, bands_all, payload, blocks)


def solution(mesh):
    in_specs = (
        P(None, ("dom", "tgt")),
        P(None, ("dom", "tgt")),
        P(("dom", "tgt")),
        P(None, ("dom", "tgt")),
        P("dom", None),
        P("dom", None, None),
        P(("dom", "tgt"), None),
        P(("dom", "tgt")),
        P(("dom", "tgt"), None),
    )
    out_specs = P(None, ("dom", "tgt"))
    return jax.shard_map(shards, mesh=mesh, in_specs=in_specs, out_specs=out_specs, check_vma=False)
```

time: 139 us -> 48.4 us (0.35)
  the two profiles are of different devices: /device:TPU:21 before, /device:TPU:1 now
where the time goes in v1:
time: 48.4 us; the launch traced here: 48.1 us
  Pallas kernels  42.4 us (88%)
  local copies, waits for them, and re-layouts  3.02 us (6%)
  other arithmetic  2.7 us (6%)
    pallas_call x1, Pallas kernels, gather_blocks(): pl.pallas_call(functools.partial(gather_kernel, n_dom, depth), out_shape=...  25.3 us
    pallas_call x1, Pallas kernels, shards(): pl.pallas_call(functools.partial(entry_kernel, n_tgt, rhs2), out_shape=ja...  17.1 us
    concatenate x1, local copies, waits for them, and re-layouts, shards(): jnp.concatenate([density, positions * wave_number, normals * wave_number,...  2.08 us

profile of v1, /device:TPU:1, one launch (start us, length us, event | category | flops | bytes accessed | tf_op | source)
XLA Modules:
  0.0 48.1 jit_solution(16233424795355508016)
XLA Ops:
  0.0 0.7 %broadcast_multiply_fusion.2 = f32[512]{0:T(512)S(1)} fusion(f32[512]{0:T(512)} %param.11), kind=kLoop, calls=%fused_computation.3 | loop fusion | flops 512 | bytes 4096 | tf_op jit(solution)/shard_map/mul | solution.py:319
  0.7 0.7 %convert_element_type.21 = f32[1,8,8]{2,1,0:T(8,128)S(1)} convert(s32[1,8,8]{2,1,0:T(8,128)} %param.14) | non-fusion elementwise | flops 64 | bytes 512 | tf_op jit(solution)/shard_map/convert_element_type | solution.py:313
  1.4 0.1 convert_element_type.22
  1.5 0.7 %broadcast_multiply_fusion = (f32[3,512]{1,0:T(4,128)S(1)}, f32[3,512]{1,0:T(4,128)S(1)}) fusion(f32[3,512]{1,0:T(4,128)} %param.10, f32[3,512]{1,0:T(4,128)} %param.9), kind=kLoop, calls=%fused_computation.1 | loop fusion | flops 3072 | bytes 24576 | tf_op jit(solution)/shard_map/mul | solution.py:318
  2.2 2.1 %concatenate.3.own_ref = f32[40,512]{1,0:T(8,128)} concatenate(f32[32,512]{1,0:T(8,128)} %param.12, f32[3,512]{1,0:T(4,128)S(1)} %get-tuple-element.6, f32[3,512]{1,0:T(4,128)S(1)} %get-tuple-element.5, f32[1,512]{1,0:T(1,128)S(1)} %bitcast.7, f32[1,512]{1,0:T(1,128)S(1)} %pad.4), dimensions={0} | concatenate | bytes 163840 | tf_op jit(solution)/shard_map/concatenate | solution.py:314
  4.3 25.3 %shard_map.91.all_ref = f32[32,40,512]{2,1,0:T(8,128)} custom-call(f32[1,40,512]{2,1,0:T(8,128)} %bitcast.5), custom_call_target="tpu_custom_call" | custom-call | tf_op jit(solution)/shard_map/pallas_call | solution.py:201
  29.6 0.8 %slice.3 = f32[16,1,64]{2,1,0:T(1,128)S(1)} slice(f32[32,40,512]{2,1,0:T(8,128)} %shard_map.91.all_ref), slice={[0:32:2], [39:40:1], [0:64:1]} | slice | bytes 8192 | tf_op jit(solution)/shard_map/slice | solution.py:325
  30.4 0.6 %convert_bitcast_fusion.band_ref = s32[16,64]{1,0:T(8,128)} fusion(f32[16,1,64]{2,0,1:T(8,128)S(1)} %bitcast.6), kind=kLoop, calls=%fused_computation | loop fusion | flops 1024 | bytes 8192 | tf_op jit(solution)/shard_map/convert_element_type | solution.py:325
  31.0 17.1 %shard_map.92 = f32[32,512]{1,0:T(8,128)} custom-call(s32[4,24]{1,0:T(4,128)} %near_ref.1, s32[4]{0:T(128)} %count_ref.1, s32[4,24]{1,0:T(4,128)} %flag_ref.1, s32[1,8]{1,0:T(1,128)} %partner_ref.1, s32[16,64]{1,0:T(8,128)} %convert_bitcast_fusion.band_ref, f32[40,512]{1,0:T(8,128)} %concatenate.3.own_ref, f32[32,40,512]{2,1,0:T(8,128)} %shard_map.91.all_ref), custom_call_target="tpu_custom_call" | custom-call | tf_op jit(solution)/shard_map/pallas_call | solution.py:328
  (1 shorter events, 0.0 us)

commit v2 on v1

--- a/solution.py
+++ b/solution.py
@@ -192,10 +192,25 @@
         each(level, finish)
 
 
+def pack_kernel(rhs2, band_ref, pos_ref, normal_ref, weight_ref, density_ref, out_ref):
+    points = out_ref.shape[-1]
+    out_ref[0, :rhs2] = density_ref[...]
+    out_ref[0, rhs2 : rhs2 + 3] = pos_ref[...] * wave_number
+    out_ref[0, rhs2 + 3 : rhs2 + 6] = normal_ref[...] * wave_number
+    out_ref[0, rhs2 + 6 : rhs2 + 7] = weight_ref[...] * (wave_number / (4.0 * math.pi))
+    _, rounds, band_size = band_ref.shape
+    lane = lax.broadcasted_iota(jnp.int32, (1, points), 1)
+    bands = jnp.zeros((1, points), jnp.int32)
+    for r in range(rounds):
+        for b in range(band_size):
+            bands = jnp.where(lane == r * band_size + b, band_ref[0, r, b], bands)
+    out_ref[0, rhs2 + 7 : rhs2 + 8] = bands.astype(jnp.float32)
+
+
 def gather_blocks(payload, n_dom, n_tgt):
-    channels, points = payload.shape
+    _, channels, points = payload.shape
     if n_tgt != 2 or n_dom % 4 or n_dom > 16 or points % (2 * TILE):
-        return lax.all_gather(payload, ("dom", "tgt"), axis=0, tiled=False)
+        return lax.all_gather(payload[0], ("dom", "tgt"), axis=0, tiled=False)
     depth = n_dom // 4
     dma = pltpu.SemaphoreType.DMA
     return pl.pallas_call(
@@ -215,24 +230,34 @@
             dma((2, 4, depth)),
             dma,
         ],
-        compiler_params=pltpu.CompilerParams(collective_id=0, has_side_effects=True),
-    )(payload[None])
+        compiler_params=pltpu.CompilerParams(collective_id=0, has_side_effects=True, vmem_limit_bytes=8 << 20),
+    )(payload)
 
 
 def entry_kernel(
-    n_tgt, rhs2, near_ref, count_ref, flag_ref, partner_ref, band_ref, own_ref, all_ref, out_ref, xb, kbuf, left
+    n_tgt, rhs2, band_size, near_ref, count_ref, flag_ref, partner_ref, own_ref, all_ref, out_ref, xb, kbuf, left, band_ref, band_sem
 ):
     local_tiles, max_near = near_ref.shape
-    band_size = band_ref.shape[1] // partner_ref.shape[1]
+    rounds = partner_ref.shape[1]
     part_tiles = local_tiles * n_tgt
     me = lax.axis_index("dom")
     half_rows = rhs2 // 2
+    copies = [
+        pltpu.make_async_copy(
+            all_ref.at[partner_ref[0, r] * n_tgt, rhs2 + 7, pl.ds(0, band_ref.shape[1])], band_ref.at[r], band_sem.at[r]
+        )
+        for r in range(rounds)
+    ]
+    for copy in copies:
+        copy.start()
     kbuf[...] = jnp.zeros_like(kbuf)
+    for copy in copies:
+        copy.wait()
 
     def one_tile(t, _):
         lanes = pl.ds(pl.multiple_of(t * TILE, TILE), TILE)
         for c in range(3):
-            row = own_ref[pl.ds(rhs2 + c, 1), lanes]
+            row = own_ref[0, pl.ds(rhs2 + c, 1), lanes]
             xb[c] = jnp.broadcast_to(row, (TILE, TILE)).T
         used = count_ref[t]
         left[...] = jnp.zeros_like(left)
@@ -241,7 +266,7 @@
             pick = near_ref[t, j]
             beyond = jnp.maximum(pick - part_tiles, 0)
             other = partner_ref[0, beyond // band_size]
-            far_tile = band_ref[other, beyond]
+            far_tile = band_ref[beyond // band_size, beyond].astype(jnp.int32)
             is_own = pick < part_tiles
             tile = jnp.where(is_own, pick, far_tile)
             dom = jnp.where(is_own, me, other)
@@ -310,32 +335,31 @@
     rhs2 = density.shape[0]
     rounds, band_size = band_list.shape[1:]
     bands = rounds * band_size
-    band_row = jnp.pad(band_list.reshape(1, bands).astype(jnp.float32), ((0, 0), (0, points - bands)))
-    payload = jnp.concatenate(
-        [
-            density,
-            positions * wave_number,
-            normals * wave_number,
-            weights[None, :] * (wave_number / (4.0 * math.pi)),
-            band_row,
-        ],
-        axis=0,
-    )
-    blocks = gather_blocks(payload, n_dom, n_tgt)
-    bands_all = blocks[::n_tgt, rhs2 + 7, :bands].astype(jnp.int32)
     smem = pl.BlockSpec(memory_space=pltpu.SMEM)
     vmem = pl.BlockSpec(memory_space=pltpu.VMEM)
+    payload = pl.pallas_call(
+        functools.partial(pack_kernel, rhs2),
+        out_shape=jax.ShapeDtypeStruct((1, rhs2 + 8, points), jnp.float32),
+        in_specs=[smem] + [vmem] * 4,
+        out_specs=vmem,
+        compiler_params=pltpu.CompilerParams(vmem_limit_bytes=4 << 20),
+    )(band_list, positions, normals, weights[None, :], density)
+    blocks = gather_blocks(payload, n_dom, n_tgt)
+    band_lanes = -(-bands // TILE) * TILE
     return pl.pallas_call(
-        functools.partial(entry_kernel, n_tgt, rhs2),
+        functools.partial(entry_kernel, n_tgt, rhs2, band_size),
         out_shape=jax.ShapeDtypeStruct((rhs2, points), jnp.float32),
-        in_specs=[smem] * 5 + [vmem] * 2,
+        in_specs=[smem] * 4 + [vmem] * 2,
         out_specs=vmem,
         scratch_shapes=[
             pltpu.VMEM((3, TILE, TILE), jnp.float32),
             pltpu.VMEM((TILE, 4 * TILE), jnp.bfloat16),
             pltpu.VMEM((rhs2, 4 * TILE), jnp.bfloat16),
+            pltpu.SMEM((rounds, band_lanes), jnp.float32),
+            pltpu.SemaphoreType.DMA((rounds,)),
         ],
-    )(near_list, near_count, singular, partners, bands_all, payload, blocks)
+        compiler_params=pltpu.CompilerParams(vmem_limit_bytes=4 * blocks.size + (6 << 20)),
+    )(near_list, near_count, singular, partners, payload, blocks)
 
 
 def solution(mesh):

time: 48.4 us -> 43 us (0.89)
  the two profiles are of different devices: /device:TPU:1 before, /device:TPU:6 now
where the time goes in v2:
time: 43 us; the launch traced here: 42.3 us
  Pallas kernels  38.6 us (90%)
  local copies, waits for them, and re-layouts  3.64 us (8%)
    pallas_call x1, Pallas kernels, gather_blocks(): pl.pallas_call(functools.partial(gather_kernel, n_dom, depth), out_shape=...  20.3 us
    pallas_call x1, Pallas kernels, shards(): pl.pallas_call(functools.partial(entry_kernel, n_tgt, rhs2, band_size), o...  17.7 us
    unnamed x18, local copies, waits for them, and re-layouts  3.64 us

profile of v2, /device:TPU:6, one launch (start us, length us, event | category | flops | bytes accessed | tf_op | source)
XLA Modules:
  0.0 42.3 jit_solution(10983106344723659843)
XLA Ops:
  0.0 0.0 copy-start.7
  0.0 0.0 copy-start.8
  0.0 0.0 copy-start
  0.0 0.9 %copy-done = f32[32,512]{1,0:T(8,128)S(1)} copy-done((f32[32,512]{1,0:T(8,128)S(1)}, f32[32,512]{1,0:T(8,128)}, u32[]{:S(2)}) %copy-start) | copy-done | bytes 65560
  0.9 0.0 copy-start.1
  0.9 0.7 %copy-done.1 = f32[3,512]{1,0:T(4,128)S(1)} copy-done((f32[3,512]{1,0:T(4,128)S(1)}, f32[3,512]{1,0:T(4,128)}, u32[]{:S(2)}) %copy-start.1) | copy-done | bytes 6168
  1.6 0.0 copy-start.2
  1.6 0.7 %copy-done.2 = f32[3,512]{1,0:T(4,128)S(1)} copy-done((f32[3,512]{1,0:T(4,128)S(1)}, f32[3,512]{1,0:T(4,128)}, u32[]{:S(2)}) %copy-start.2) | copy-done | bytes 6168
  2.3 0.0 copy-start.3
  2.3 0.7 %copy-done.3 = s32[1,8,8]{2,1,0:T(8,128)S(1)} copy-done((s32[1,8,8]{2,1,0:T(8,128)S(1)}, s32[1,8,8]{2,1,0:T(8,128)}, u32[]{:S(2)}) %copy-start.3) | copy-done | bytes 280
  3.0 0.0 copy-start.4
  3.0 0.7 %copy-done.4 = f32[512]{0:T(512)S(1)} copy-done((f32[512]{0:T(512)S(1)}, f32[512]{0:T(512)}, u32[]{:S(2)}) %copy-start.4) | copy-done | bytes 2072
  3.6 0.0 copy-start.5
  3.6 0.0 copy-start.6
  3.6 0.6 %shard_map.91.own_ref = f32[1,40,512]{2,1,0:T(8,128)S(1)} custom-call(s32[1,8,8]{2,1,0:T(8,128)S(1)} %copy-done.3, f32[3,512]{1,0:T(4,128)S(1)} %copy-done.1, f32[3,512]{1,0:T(4,128)S(1)} %copy-done.2, f32[1,512]{1,0:T(1,128)S(1)} %bitcast.1, f32[32,512]{1,0:T(8,128)S(1)} %copy-done), custom_call_target="tpu_custom_call" | custom-call | tf_op jit(solution)/shard_map/pallas_call | solution.py:340
  4.3 20.3 %shard_map.92.all_ref = f32[32,40,512]{2,1,0:T(8,128)S(1)} custom-call(f32[1,40,512]{2,1,0:T(8,128)S(1)} %shard_map.91.own_ref), custom_call_target="tpu_custom_call" | custom-call | tf_op jit(solution)/shard_map/pallas_call | solution.py:216
  24.6 0.0 copy-done.7
  24.6 0.0 copy-done.8
  24.6 0.0 copy-done.5
  24.6 0.0 copy-done.6
  24.7 17.7 %shard_map.93 = f32[32,512]{1,0:T(8,128)} custom-call(s32[4,24]{1,0:T(4,128)S(1)} %copy-done.5, s32[4]{0:T(128)S(1)} %copy-done.7, s32[4,24]{1,0:T(4,128)S(1)} %copy-done.6, s32[1,8]{1,0:T(1,128)S(1)} %copy-done.8, f32[1,40,512]{2,1,0:T(8,128)S(1)} %shard_map.91.own_ref, f32[32,40,512]{2,1,0:T(8,128)S(1)} %shard_map.92.all_ref), custom_call_target="tpu_custom_call" | custom-call | tf_op jit(solution)/shard_map/pallas_call | solution.py:349
Async XLA Ops:
  0.0 24.6 %copy-start.7 = (s32[4]{0:T(128)S(1)}, s32[4]{0:T(128)}, u32[]{:S(2)}) copy-start(s32[4]{0:T(128)} %count_ref.1) | copy-start | bytes 52
  0.0 24.6 %copy-start.8 = (s32[1,8]{1,0:T(1,128)S(1)}, s32[1,8]{1,0:T(1,128)}, u32[]{:S(2)}) copy-start(s32[1,8]{1,0:T(1,128)} %partner_ref.1) | copy-start | bytes 100
  0.0 0.9 %copy-start = (f32[32,512]{1,0:T(8,128)S(1)}, f32[32,512]{1,0:T(8,128)}, u32[]{:S(2)}) copy-start(f32[32,512]{1,0:T(8,128)} %density_ref.1) | copy-start | bytes 196612
  0.9 0.7 %copy-start.1 = (f32[3,512]{1,0:T(4,128)S(1)}, f32[3,512]{1,0:T(4,128)}, u32[]{:S(2)}) copy-start(f32[3,512]{1,0:T(4,128)} %pos_ref.1) | copy-start | bytes 18436
  1.6 0.7 %copy-start.2 = (f32[3,512]{1,0:T(4,128)S(1)}, f32[3,512]{1,0:T(4,128)}, u32[]{:S(2)}) copy-start(f32[3,512]{1,0:T(4,128)} %normal_ref.1) | copy-start | bytes 18436
  2.3 0.7 %copy-start.3 = (s32[1,8,8]{2,1,0:T(8,128)S(1)}, s32[1,8,8]{2,1,0:T(8,128)}, u32[]{:S(2)}) copy-start(s32[1,8,8]{2,1,0:T(8,128)} %band_ref.1) | copy-start | bytes 772
  3.0 0.7 %copy-start.4 = (f32[512]{0:T(512)S(1)}, f32[512]{0:T(512)}, u32[]{:S(2)}) copy-start(f32[512]{0:T(512)} %param.11) | copy-start | bytes 6148
  3.6 21.0 %copy-start.5 = (s32[4,24]{1,0:T(4,128)S(1)}, s32[4,24]{1,0:T(4,128)}, u32[]{:S(2)}) copy-start(s32[4,24]{1,0:T(4,128)} %near_ref.1) | copy-start | bytes 1156
  3.6 21.0 %copy-start.6 = (s32[4,24]{1,0:T(4,128)S(1)}, s32[4,24]{1,0:T(4,128)}, u32[]{:S(2)}) copy-start(s32[4,24]{1,0:T(4,128)} %flag_ref.1) | copy-start | bytes 1156
